TPU v7x, 128 devices: a whole 4x4x4 slice. The times are simulated.
128 devices in a mesh: prompt: 4 (over x), dp: 4 (over y), mp: 8 (over z, core).
Axes of the slice: x: 4, y: 4, z: 4, core: 2. Of those that a mesh axis runs over, the one named last changes fastest.
Arguments:
- prompts: bfloat16 [8, 100, 4096], P('prompt'), may hold values from -6 to 6
- target_embed: bfloat16 [4, 512, 4096], P('dp'), may hold values from -6 to 6
- labels: int32 [4, 512], P('dp'), may hold values from 0 to 16383
- lengths: int32 [4], P('dp'), may hold values from 128 to 512
- attn_gain: float32 [4096], replicated, may hold values from 0.5 to 1.5
- w_qkv: bfloat16 [3, 4096, 2048], P(None, None, 'mp'), may hold values from -4 to 4
- w_out: bfloat16 [2048, 4096], P('mp'), may hold values from -0.5 to 0.5
- final_gain: float32 [4096], replicated, may hold values from 0.5 to 1.5
- w_vocab: bfloat16 [4096, 16384], P(None, ('dp', 'mp')), may hold values from -3 to 3
Outputs:
- token_loss: float32 [8, 4, 512], P('prompt', 'dp')
- prompt_loss: float32 [8], replicated
Inputs may be any that keep to these rules, and one draw needn't show every extreme that they name: `lengths`: positions from a sequence's length on are padding.
All inputs are finite; a program needn't handle non-finite values.
Results may differ from a plain program's by a relative error of at most 0.006.
Values may be sent and summed in bfloat16 or wider, within the bound.
No kernel may reach another device: no remote copies, remote signals or barrier semaphores. Data moves between devices by JAX's collectives and lax.ppermute only.
A program may use at most 128 MiB of HBM per device.

v0:
```python
import math
import jax
import jax.numpy as jnp
from jax import lax
from jax.sharding import Mesh
from jax.sharding import PartitionSpec as P

HD = 128
MP = ("mp_0", "mp_1")
DP_MP = ("dp", "mp_0", "mp_1")
EPSILON = 1e-05
BASE_THETA = 10000.0


def collected_together(value, axis):
    leaves = jax.tree.leaves(value)
    order = sorted(range(len(leaves)), key=lambda k: -leaves[k].size)
    width = (1, *leaves[order[0]].shape)[-1]
    lines = [
        jnp.pad(leaves[k].reshape(-1), (0, -leaves[k].size % width)).reshape(-1, width)
        for k in order
    ]
    both, at, found = (lax.all_gather(jnp.concatenate(lines), axis), 0, {})
    for k, line in zip(order, lines):
        slab = both[:, at : at + len(line)].reshape(len(both), -1)
        found[k] = slab[:, : leaves[k].size].reshape(-1, *leaves[k].shape)
        at += len(line)
    numbers = iter(range(len(leaves)))
    return jax.tree.map(lambda _: found[next(numbers)], value)


def merged_by_axis(value, axes, combine):
    for axis in axes:
        pieces = collected_together(
            jax.tree.map(
                lambda part, kind: part.astype(kind),
                value,
                jax.tree.map(lambda a: jnp.bfloat16 if a.dtype == jnp.float32 else a.dtype, value),
            ),
            axis,
        )
        widened = [
            jax.tree.map(lambda part, own: part[k].astype(own.dtype), pieces, value)
            for k in range(lax.axis_size(axis))
        ]
        value = widened[0]
        for other in widened[1:]:
            value = combine(value, other)
    return value


def sent_to_all(value, axis):
    copies = jnp.broadcast_to(value, (lax.axis_size(axis), *value.shape))
    return lax.all_to_all(copies, axis, split_axis=0, concat_axis=0, tiled=True)


def of_everyone(value, axis):
    everything = sent_to_all(value, axis)
    return jnp.sum(everything, axis=0)


def rms_scaled(values, gain_vec):
    widened = values.astype(jnp.float32)
    return (
        widened
        * lax.rsqrt(jnp.mean(widened * widened, axis=-1, keepdims=True) + EPSILON)
        * gain_vec
    )


def rotate(values, offset, head_dim):
    number_rows = values.shape[-2]
    full_width = values.shape[-1]
    per_head = values.reshape(values.shape[:-1] + (full_width // head_dim, head_dim))
    half_dim = head_dim // 2
    positions = (offset + jnp.arange(number_rows, dtype=jnp.int32)).astype(jnp.float32)
    indices_f = jnp.arange(half_dim, dtype=jnp.int32).astype(jnp.float32)
    frequency = jnp.exp(indices_f * (-2.0 * math.log(BASE_THETA) / head_dim))
    angles = positions[:, None] * frequency[None, :]
    cosine = jnp.cos(angles)[:, None, :]
    sine_part = jnp.sin(angles)[:, None, :]
    first_half = per_head[..., :half_dim]
    second_half = per_head[..., half_dim:]
    turned = jnp.concatenate(
        [
            first_half * cosine - second_half * sine_part,
            second_half * cosine + first_half * sine_part,
        ],
        axis=-1,
    )
    return turned.reshape(values.shape)


def project(normed, weights, offset, rotated_count):
    lead_shape = normed.shape[:-1]
    flat_rows = normed.reshape(-1, normed.shape[-1])
    stacked = jnp.einsum("nd,cde->cne", flat_rows, weights, preferred_element_type=jnp.float32)
    stacked = stacked.reshape((weights.shape[0],) + lead_shape + (weights.shape[2],))
    results = []
    for index_w in range(weights.shape[0]):
        product = stacked[index_w]
        if index_w < rotated_count:
            product = rotate(product, offset, HD)
        results.append(product.astype(jnp.bfloat16))
    return tuple(results)


def attend(prompt_keys, prompt_vals, target_q, target_k, target_v):
    seq_count = target_q.shape[0]
    target_len = target_q.shape[1]
    prompt_len = prompt_keys.shape[0]
    heads_here = target_q.shape[2] // HD
    keys_all = jnp.concatenate([prompt_keys[None], target_k], axis=1)
    vals_all = jnp.concatenate([prompt_vals[None], target_v], axis=1)
    query_h = target_q.reshape(seq_count, target_len, heads_here, HD)
    key_h = keys_all.reshape(seq_count, prompt_len + target_len, heads_here, HD)
    val_h = vals_all.reshape(seq_count, prompt_len + target_len, heads_here, HD)
    scores = jnp.einsum(
        "bqhe,bkhe->bhqk", query_h, key_h, preferred_element_type=jnp.float32
    ) * HD ** (-0.5)
    key_index = jnp.arange(prompt_len + target_len, dtype=jnp.int32)
    query_pos = prompt_len + jnp.arange(target_len, dtype=jnp.int32)
    allowed = key_index[None, :] <= query_pos[:, None]
    scores = jnp.where(allowed[None, None], scores, -1e30)
    top_val = jnp.max(scores, axis=-1, keepdims=True)
    expo = jnp.exp(scores - top_val)
    probs = (expo / jnp.sum(expo, axis=-1, keepdims=True)).astype(jnp.bfloat16)
    context = jnp.einsum("bhqk,bkhe->bqhe", probs, val_h, preferred_element_type=jnp.float32)
    return context.astype(jnp.bfloat16).reshape(seq_count, target_len, heads_here * HD)


def block_stats(normed_rows, label_ids, columns, column_ids):
    logits = jnp.dot(normed_rows, columns, preferred_element_type=jnp.float32)
    top_val = jnp.max(logits, axis=1)
    sum_exp = jnp.sum(jnp.exp(logits - top_val[:, None]), axis=1)
    picked = jnp.sum(jnp.where(column_ids[None, :] == label_ids[:, None], logits, 0.0), axis=1)
    return (top_val, sum_exp, picked)


def combine_stats(earlier, later):
    top_val = jnp.maximum(earlier[0], later[0])
    sum_exp = earlier[1] * jnp.exp(earlier[0] - top_val) + later[1] * jnp.exp(later[0] - top_val)
    return (top_val, sum_exp, earlier[2] + later[2])


def shards(prompts, target_embed, labels, lengths, attn_gain, w_qkv, w_out, final_gain, w_vocab):
    n_prompt = lax.axis_size("prompt")
    n_model = lax.axis_size(MP)
    prompts_here = prompts.shape[0]
    prompt_len = prompts.shape[1]
    seq_count = target_embed.shape[0]
    target_len = target_embed.shape[1]
    model_width = target_embed.shape[2]
    normed_target = rms_scaled(target_embed, attn_gain).astype(jnp.bfloat16)
    target_q, target_k, target_v = project(normed_target, w_qkv, prompt_len, 2)
    normed_prompts = rms_scaled(prompts, attn_gain).astype(jnp.bfloat16)
    prompt_k, prompt_v = project(normed_prompts, w_qkv[1:], 0, 1)

    def one_prompt(pair):
        return attend(pair[0], pair[1], target_q, target_k, target_v)

    contexts = lax.map(one_prompt, (prompt_k, prompt_v))
    ctx_rows = contexts.reshape(-1, contexts.shape[-1])
    total_rows = ctx_rows.shape[0]
    keep_rows = total_rows // n_model
    row_context = lax.all_to_all(ctx_rows, MP, split_axis=0, concat_axis=1, tiled=True)
    full_out = lax.all_gather(w_out, MP, axis=0, tiled=True)
    group_width = w_out.shape[0]
    grouped = jnp.einsum(
        "rgk,gkd->rgd",
        row_context.reshape(keep_rows, n_model, group_width),
        full_out.reshape(n_model, group_width, model_width),
        preferred_element_type=jnp.float32,
    )
    attn_part = jnp.sum(grouped.astype(jnp.bfloat16).astype(jnp.float32), axis=1)
    my_start = lax.axis_index(MP) * keep_rows
    embed_rows = jnp.tile(target_embed.reshape(-1, model_width), (prompts_here, 1))
    residual = lax.dynamic_slice_in_dim(embed_rows, my_start, keep_rows, 0).astype(jnp.float32)
    label_rows = lax.dynamic_slice_in_dim(
        jnp.tile(labels.reshape(-1), prompts_here), my_start, keep_rows, 0
    )
    hidden = residual + attn_part
    normed_out = rms_scaled(hidden, final_gain).astype(jnp.bfloat16)
    vocab_cols = w_vocab.shape[1]
    every_rows, every_labels = (
        lax.all_gather(normed_out, DP_MP, axis=0, tiled=True),
        lax.all_gather(label_rows, DP_MP, axis=0, tiled=True),
    )
    block_index = lax.axis_index("dp") * n_model + lax.axis_index(MP)
    column_ids = block_index * vocab_cols + jnp.arange(vocab_cols, dtype=jnp.int32)
    local_stats = block_stats(every_rows, every_labels, w_vocab, column_ids)
    merged = merged_by_axis(local_stats, DP_MP, combine_stats)
    group_start = lax.axis_index("dp") * total_rows
    merged = tuple(
        (lax.dynamic_slice_in_dim(member, group_start, total_rows, 0) for member in merged)
    )
    losses = (merged[0] + jnp.log(merged[1]) - merged[2]).reshape(
        prompts_here, seq_count, target_len
    )
    valid = jnp.arange(target_len, dtype=jnp.int32)[None, :] < lengths[:, None]
    token_loss = jnp.where(valid[None], losses, 0.0)
    prompt_sums = jnp.sum(token_loss, axis=(1, 2))
    all_prompts = prompts_here * n_prompt
    slot_ids = lax.axis_index("prompt") * prompts_here + jnp.arange(prompts_here, dtype=jnp.int32)
    placed = jnp.sum(
        jnp.where(
            jnp.arange(all_prompts, dtype=jnp.int32)[:, None] == slot_ids[None, :],
            prompt_sums[None, :],
            0.0,
        ),
        axis=1,
    )
    valid_here = jnp.sum(lengths).astype(jnp.float32)
    totals, counted = (
        of_everyone(placed, ("prompt", "dp")),
        of_everyone(valid_here, ("prompt", "dp")),
    )
    prompt_loss = totals * float(n_prompt) / counted
    return (token_loss, prompt_loss)


def solution(mesh):
    finer = Mesh(
        mesh.devices.reshape(mesh.shape["prompt"], mesh.shape["dp"], 4, 2),
        ("prompt", "dp", "mp_0", "mp_1"),
    )
    return jax.shard_map(
        shards,
        mesh=finer,
        in_specs=(
            P("prompt", None, None),
            P("dp", None, None),
            P("dp", None),
            P("dp"),
            P(),
            P(None, None, MP),
            P(MP, None),
            P(),
            P(None, DP_MP),
        ),
        out_specs=(P("prompt", "dp", None), P()),
        check_vma=False,
    )
```

profile of v0, /device:TPU:0, one launch (start us, length us, event | category | flops | bytes accessed | tf_op | source)
XLA Modules:
  0.0 313.7 jit_solution(16696660986336960218)
XLA Ops:
  7.2 0.7 all-gather.10.cloned.1.call-update
  7.9 3.2 %fusion.36 = f32[2,100]{0,1:T(8,128)S(1)} fusion(bf16[2,100,4096]{2,0,1:T(2,128)(2,1)} %param.11), kind=kLoop, calls=%fused_computation.40 | loop fusion | flops 2457400 | bytes 1639200 | tf_op jit(solution)/shard_map/reduce_sum | solution.py:66
  11.2 2.4 fusion.38
  13.6 1.0 copy.72
  14.6 0.3 reshape.1004
  14.9 3.2 %fusion.42 = f32[2,200,256]{2,1,0:T(8,128)S(1)} fusion(bf16[200,4096,1]{1,0,2:T(8,128)(2,1)S(1)} %reshape.1004, bf16[3,4096,256]{2,1,0:T(8,128)(2,1)} %param.16), kind=kOutput, calls=%fused_computation.47 | convolution fusion | flops 838860800 | bytes 6242304 | tf_op jit(solution)/shard_map/nd,cde->cne/dot_general | solution.py:97
  18.2 3.2 %fusion.26 = f32[512]{0:T(512)S(1)} fusion(bf16[1,512,4096]{2,1,0:T(8,128)(2,1)} %param.12), kind=kLoop, calls=%fused_computation.27 | loop fusion | flops 6290944 | bytes 4196352 | tf_op jit(solution)/shard_map/reduce_sum | solution.py:66
  21.5 0.7 copy-done.1
  22.2 6.4 %fusion.39 = f32[3,512,256]{1,2,0:T(8,128)S(1)} fusion(bf16[3,4096,256]{2,1,0:T(8,128)(2,1)} %param.16, bf16[1,512,4096]{2,1,0:T(8,128)(2,1)S(1)} %copy-done.1, f32[4096]{0:T(1024)S(1)} %copy-done.7, f32[512]{0:T(512)S(1)} %add_rsqrt_fusion.1), kind=kOutput, calls=%fused_computation.46 | convolution fusion | flops 3229614080 | bytes 12077056 | tf_op jit(solution)/shard_map/nd,cde->cne/dot_general | solution.py:97
  28.7 0.5 multiply_cosine_fusion
  29.3 0.1 fusion.104
  29.3 0.2 subtract_convert_fusion
  29.6 0.1 copy.84
  29.7 0.1 reshape.1007
  29.8 0.1 reshape_squeeze.9
  29.9 0.3 multiply_cosine_fusion.1
  30.2 0.4 subtract_convert_fusion.2
  30.6 0.3 pad_maximum_fusion.4
  30.9 0.1 copy.83
  31.1 8.7 %while.11 = (s32[]{:T(128)}, bf16[2,1,512,256]{3,2,0,1:T(8,128)(2,1)}, bf16[2,100,256]{2,1,0:T(8,128)(2,1)S(1)}, bf16[1,512,256]{1,2,0:T(8,128)(2,1)S(1)}, bf16[...) while((s32[]{:T(128)}, ...), condition=%wide.wide.region_5.6_spmd, body=%wide.wide.region_2.5_spmd.sunk | while | flops 488637120 | bytes 5288549 | solution.py:162
  31.1 0.1 copy.116
  31.3 0.3 pad_maximum_fusion.7
  31.6 0.2 iota_compare_fusion.4
  31.8 1.2 fusion.133
  33.0 1.6 fusion.134
  34.6 0.1 copy.117
  34.7 0.7 constant_dynamic-update-slice_fusion.3
  35.4 0.1 copy.116
  35.6 0.3 pad_maximum_fusion.7
  35.9 0.2 iota_compare_fusion.4
  36.1 1.2 fusion.133
  37.3 1.6 fusion.134
  38.9 0.1 copy.117
  39.0 0.7 constant_dynamic-update-slice_fusion.3
  39.7 5.8 %all-to-all-start = ((bf16[8,128,256]{2,1,0:T(8,128)(2,1)}), bf16[8,128,256]{2,1,0:T(8,128)(2,1)S(1)}, u32[]{:S(2)}, u32[]{:S(2)}) async-start(bf16[8,128,256]{2,1,0:T(8,128)(2,1)} %bitcast.18), calls=%async_computation | async-start | bytes 1048576 | tf_op jit(solution)/shard_map/all_to_all | solution.py:166
  45.6 16.2 %all-to-all-done = bf16[8,128,256]{2,1,0:T(8,128)(2,1)S(1)} async-done(((bf16[8,128,256]{2,1,0:T(8,128)(2,1)}), bf16[8,128,256]{2,1,0:T(8,128)(2,1)S(1)}, u32[]{:S(2)}, u32[]{:S(2)}) %all-to-all-start) | async-done | bytes 524320 | tf_op jit(solution)/shard_map/all_to_all | solution.py:166
  61.8 41.2 %all-gather.10.cloned.1.call-done = bf16[2048,4096]{1,0:T(8,128)(2,1)} async-done(((bf16[256,4096]{1,0:T(8,128)(2,1)}), bf16[2048,4096]{1,0:T(8,128)(2,1)}) %all-gather.10.cloned.1.call-update) | async-done | bytes 16777232 | tf_op jit(solution)/shard_map/all_gather | solution.py:167
  103.0 8.6 %convert_reduce_fusion = f32[128,4096]{1,0:T(8,128)S(1)} fusion(bf16[8,256,4096]{2,1,0:T(8,128)(2,1)} %bitcast.276, bf16[8,128,256]{2,1,0:T(8,128)(2,1)} %copy-done.4), kind=kOutput, calls=%fused_computation.24 | convolution fusion | flops 2159542272 | bytes 19398656 | tf_op jit(solution)/shard_map/rgk,gkd->rgd/dot_general | solution.py:169
  111.7 4.3 %tile.21 = bf16[2,512,4096]{2,1,0:T(8,128)(2,1)} broadcast(bf16[512,4096]{1,0:T(8,128)(2,1)S(1)} %bitcast.275), dimensions={1,2} | broadcast | bytes 12582912 | tf_op jit(solution)/shard_map/tile | solution.py:177
  116.0 1.6 multiply_reduce_fusion
  117.6 2.6 multiply_convert_fusion
  120.9 0.6 broadcast_in_dim.64
  121.5 6.8 %all-to-all-start.2 = ((f32[16,1,1]{2,1,0:T(1,128)}), f32[16,1,1]{2,1,0:T(1,128)S(1)}, u32[]{:S(2)}, u32[]{:S(2)}) async-start(f32[16,1,1]{2,1,0:T(1,128)} %broadcast_in_dim.64), calls=%async_computation.2 | async-start | bytes 16384 | tf_op jit(solution)/shard_map/all_to_all | solution.py:54
  128.3 0.1 dynamic-slice_bitcast_fusion
  128.4 21.5 %all-gather.3 = s32[32,1,128]{2,1,0:T(1,128)S(1)} all-gather(s32[1,1,128]{2,1,0:T(1,128)S(1)} %dynamic-slice_bitcast_fusion), channel_id=1, replica_groups=mesh['prompt'=4,'dp'=4,'mp_0'=4,'mp_1'=2] {'dp','mp_0','mp_1'}, dimensions={0}, use_global_device_ids=true | all-gather | bytes 16896 | tf_op jit(solution)/shard_map/all_gather | solution.py:187
  149.9 84.9 %all-gather.12.cloned.1.call-done = bf16[4096,4096]{1,0:T(8,128)(2,1)} async-done(((bf16[128,4096]{1,0:T(8,128)(2,1)}), bf16[4096,4096]{1,0:T(8,128)(2,1)}) %all-gather.12.cloned.1.call-update) | async-done | bytes 33554448 | tf_op jit(solution)/shard_map/all_gather | solution.py:186
  234.8 24.1 %fusion.105 = (f32[4096]{0:T(1024)S(1)}, f32[4096,512]{0,1:T(8,128)}) fusion(bf16[4096,4096]{1,0:T(8,128)(2,1)} %all-gather.12.cloned.1.call-done, bf16[4096,512]{1,0:T(8,128)(2,1)} %param.19), kind=kOutput, calls=%fused_computation.174 | convolution fusion | flops 17181962240 | bytes 46153728 | tf_op jit(solution)/shard_map/dot_general | solution.py:133
  258.9 4.6 %exponential_reduce_fusion = (bf16[4096]{0:T(1024)(128)(2,1)S(1)}, bf16[4096]{0:T(1024)(128)(2,1)S(1)}) fusion(f32[4096,512]{0,1:T(8,128)} %get-tuple-element.134, f32[4096]{0:T(1024)S(1)} %get-tuple-element.133, s32[4096]{0:T(1024)S(1)} %bitcast.292, s32[512]{0:T(512)S(1)} %iota_add_fusion.1), kind=kLoop, calls=%fused_computation.31 | loop fusion | flops 10477568 | bytes 8439808 | tf_op jit(solution)/shard_map/reduce_sum | solution.py:135
  263.5 0.1 maximum_bitcast_fusion
  263.5 12.3 %all-gather.4 = bf16[4,3,4096]{2,1,0:T(4,128)(2,1)S(1)} all-gather(bf16[1,3,4096]{2,1,0:T(4,128)(2,1)S(1)} %maximum_bitcast_fusion), channel_id=2, replica_groups=mesh['prompt'=4,'dp'=4,'mp_0'=4,'mp_1'=2] {'dp'}, dimensions={0}, use_global_device_ids=true | all-gather | bytes 122880 | tf_op jit(solution)/shard_map/all_gather | solution.py:23
  275.8 0.2 maximum_convert_fusion.1
  276.0 0.1 fusion.70
  276.2 12.0 %all-gather.5 = bf16[4,3,4096]{2,1,0:T(4,128)(2,1)S(1)} all-gather(bf16[1,3,4096]{2,1,0:T(4,128)(2,1)S(1)} %maximum_bitcast_fusion.1), channel_id=3, replica_groups=mesh['prompt'=4,'dp'=4,'mp_0'=4,'mp_1'=2] {'mp_0'}, dimensions={0}, use_global_device_ids=true | all-gather | bytes 122880 | tf_op jit(solution)/shard_map/all_gather | solution.py:23
  288.2 0.2 maximum_convert_fusion
  288.4 0.1 fusion.48
  288.5 1.9 all-gather.6
  290.4 0.1 slice_convert_fusion.5
  290.5 0.6 fusion.100
  291.1 0.1 fusion.99
  291.2 0.6 broadcast_in_dim.59
  291.8 6.3 %all-to-all-start.1 = ((f32[16,1,8]{2,1,0:T(1,128)}), f32[16,1,8]{2,1,0:T(1,128)S(1)}, u32[]{:S(2)}, u32[]{:S(2)}) async-start(f32[16,1,8]{2,1,0:T(1,128)} %broadcast_in_dim.59), calls=%async_computation.1 | async-start | bytes 16384 | tf_op jit(solution)/shard_map/all_to_all | solution.py:54
  298.2 0.6 reduce_sum.112
  298.8 6.9 %all-to-all-done.1 = f32[16,1,8]{2,1,0:T(1,128)S(1)} async-done(((f32[16,1,8]{2,1,0:T(1,128)}), f32[16,1,8]{2,1,0:T(1,128)S(1)}, u32[]{:S(2)}, u32[]{:S(2)}) %all-to-all-start.1) | async-done | bytes 544 | tf_op jit(solution)/shard_map/all_to_all | solution.py:54
  305.8 1.1 multiply_divide_fusion
  (55 shorter events, 0.6 us)
Async XLA Ops:
  7.2 121.1 %copy-start = (s32[1,512]{1,0:T(1,128)S(1)}, s32[1,512]{1,0:T(1,128)}, u32[]{:S(2)}) copy-start(s32[1,512]{1,0:T(1,128)} %param.13) | copy-start | bytes 6148
  7.2 4.0 %copy-start.3 = (bf16[2,100,4096]{2,0,1:T(2,128)(2,1)S(1)}, bf16[2,100,4096]{2,0,1:T(2,128)(2,1)}, u32[]{:S(2)}) copy-start(bf16[2,100,4096]{2,0,1:T(2,128)(2,1)} %param.11) | copy-start | bytes 4915204
  7.2 4.0 %copy-start.7 = (f32[4096]{0:T(1024)S(1)}, f32[4096]{0:T(1024)}, u32[]{:S(2)}) copy-start(f32[4096]{0:T(1024)} %param.15) | copy-start | bytes 49156
  7.2 95.8 %all-gather.10.cloned.1.call-start = ((), (), s32[]{:S(2)}) async-start(), calls=%async_computation.3 | async-start | bytes 18874368 | tf_op jit(solution)/shard_map/all_gather | solution.py:167
  18.2 10.5 %copy-start.6 = (f32[2,200,256]{2,1,0:T(8,128)}, f32[2,200,256]{2,1,0:T(8,128)S(1)}, u32[]{:S(2)}) copy-start(f32[2,200,256]{2,1,0:T(8,128)S(1)} %fusion.42) | copy-start | bytes 1228804
  18.2 4.0 %copy-start.1 = (bf16[1,512,4096]{2,1,0:T(8,128)(2,1)S(1)}, bf16[1,512,4096]{2,1,0:T(8,128)(2,1)}, u32[]{:S(2)}) copy-start(bf16[1,512,4096]{2,1,0:T(8,128)(2,1)} %param.12) | copy-start | bytes 12582916
  28.7 1.1 slice-start
  29.7 1.4 copy-start.5
  39.7 22.1 %all-to-all-start = ((bf16[8,128,256]{2,1,0:T(8,128)(2,1)}), bf16[8,128,256]{2,1,0:T(8,128)(2,1)S(1)}, u32[]{:S(2)}, u32[]{:S(2)}) async-start(bf16[8,128,256]{2,1,0:T(8,128)(2,1)} %bitcast.18), calls=%async_computation | async-start | bytes 1048576 | tf_op jit(solution)/shard_map/all_to_all | solution.py:166
  45.5 189.3 %all-gather.12.cloned.1.call-start = ((), (), s32[]{:S(2)}) async-start(), calls=%async_computation.4 | async-start | bytes 34603008 | tf_op jit(solution)/shard_map/all_gather | solution.py:186
  61.8 41.2 %copy-start.4 = (bf16[8,128,256]{2,1,0:T(8,128)(2,1)}, bf16[8,128,256]{2,1,0:T(8,128)(2,1)S(1)}, u32[]{:S(2)}) copy-start(bf16[8,128,256]{2,1,0:T(8,128)(2,1)S(1)} %all-to-all-done) | copy-start | bytes 1572868
  103.0 8.6 %copy-start.2 = (bf16[1,512,4096]{2,1,0:T(8,128)(2,1)S(1)}, bf16[1,512,4096]{2,1,0:T(8,128)(2,1)}, u32[]{:S(2)}) copy-start(bf16[1,512,4096]{2,1,0:T(8,128)(2,1)} %param.12) | copy-start | bytes 12582916
  111.7 5.9 %copy-start.8 = (f32[4096]{0:T(1024)S(1)}, f32[4096]{0:T(1024)}, u32[]{:S(2)}) copy-start(f32[4096]{0:T(1024)} %param.18) | copy-start | bytes 49156
  121.5 169.7 %all-to-all-start.2 = ((f32[16,1,1]{2,1,0:T(1,128)}), f32[16,1,1]{2,1,0:T(1,128)S(1)}, u32[]{:S(2)}, u32[]{:S(2)}) async-start(f32[16,1,1]{2,1,0:T(1,128)} %broadcast_in_dim.64), calls=%async_computation.2 | async-start | bytes 16384 | tf_op jit(solution)/shard_map/all_to_all | solution.py:54
  291.8 13.9 %all-to-all-start.1 = ((f32[16,1,8]{2,1,0:T(1,128)}), f32[16,1,8]{2,1,0:T(1,128)S(1)}, u32[]{:S(2)}, u32[]{:S(2)}) async-start(f32[16,1,8]{2,1,0:T(1,128)} %broadcast_in_dim.59), calls=%async_computation.1 | async-start | bytes 16384 | tf_op jit(solution)/shard_map/all_to_all | solution.py:54
Sparse Core Ops, SparseCore 0:
  9.7 93.2 all-gather.9
  120.4 114.3 all-gather.11
where the time goes:
time: 314 us
  waiting for transfers between devices  150 us (48%)
  matrix products  47.8 us (15%)
  blocking collectives  47.6 us (15%)
  other arithmetic  23.8 us (8%)
  starting transfers between devices  19 us (6%)
  between operations  15.1 us (5%)
  local copies, waits for them, and re-layouts  10.3 us (3%)
    all_gather x1, waiting for transfers between devices, shards(): lax.all_gather(normed_out, DP_MP, axis=0, tiled=True)  84.9 us
    all_gather x1, waiting for transfers between devices, shards(): full_out = lax.all_gather(w_out, MP, axis=0, tiled=True)  41.2 us
    all_gather x3, blocking collectives, collected_together(): both, at, found = (lax.all_gather(jnp.concatenate(lines), axis), 0, {})  26.1 us
    dot_general x1, matrix products, block_stats(): logits = jnp.dot(normed_rows, columns, preferred_element_type=jnp.float32)  24.1 us
    all_gather x1, blocking collectives, shards(): lax.all_gather(label_rows, DP_MP, axis=0, tiled=True)  21.5 us
    all_to_all x1, waiting for transfers between devices, shards(): lax.all_to_all(ctx_rows, MP, split_axis=0, concat_axis=1, tiled=True)  16.2 us
    all_to_all x2, starting transfers between devices, sent_to_all(): return lax.all_to_all(copies, axis, split_axis=0, concat_axis=0, tiled=True)  13.1 us
    dot_general x2, matrix products, project(): jnp.einsum('nd,cde->cne', flat_rows, weights, preferred_element_type=jnp....  9.64 us
  transfers between devices with their start and end apart: 5, of which 4 were waited for; matrix products, arithmetic and copies ran while one was open for 20% of the time, Pallas kernels for 0%

commit v1 on v0

--- a/solution.py
+++ b/solution.py
@@ -164,7 +164,9 @@
     total_rows = ctx_rows.shape[0]
     keep_rows = total_rows // n_model
     row_context = lax.all_to_all(ctx_rows, MP, split_axis=0, concat_axis=1, tiled=True)
-    full_out = lax.all_gather(w_out, MP, axis=0, tiled=True)
+    full_out = jnp.concatenate(
+        lax.all_to_all(jnp.stack([w_out] * lax.axis_size(MP)), MP, 0, 0), axis=0
+    )
     group_width = w_out.shape[0]
     grouped = jnp.einsum(
         "rgk,gkd->rgd",

time: 314 us -> 459 us (1.46)
  waiting for transfers between devices: 150 us -> 275 us
  blocking collectives: 47.6 us -> 63.1 us
  local copies, waits for them, and re-layouts: 10.3 us -> 15 us
    all_to_all x1, waiting for transfers between devices: 16.2 us -> 184 us  [shards(): lax.all_to_all(jnp.stack([w_out] * lax.axis_size(MP)), MP, 0, 0)]
    all_gather x1 -> x0, waiting for transfers between devices: 41.2 us -> none  [shards(): full_out = lax.all_gather(w_out, MP, axis=0, tiled=True)]
    all_to_all x0 -> x1, blocking collectives: none -> 15.7 us  [shards(): lax.all_to_all(ctx_rows, MP, split_axis=0, concat_axis=1, tiled=True)]
    another operation x1 -> x2, local copies, waits for them, and re-layouts: 0.07 us -> 6.94 us  [the longest x1 6.87 us: shards(): jnp.stack([w_out] * lax.axis_size(MP))]
  transfers between devices with their start and end apart: 5 -> 4, of which waited for: 4 -> 3; matrix products, arithmetic and copies ran while one was open for 20% -> 7% of each run, Pallas kernels for 0% -> 0%
where the time goes in v1:
time: 459 us; the launch traced here: 458 us
  waiting for transfers between devices  275 us (60%)
  blocking collectives  63.1 us (14%)
  matrix products  47.6 us (10%)
  other arithmetic  22.7 us (5%)
  starting transfers between devices  19.4 us (4%)
  between operations  15.1 us (3%)
  local copies, waits for them, and re-layouts  15 us (3%)
    all_to_all x1, waiting for transfers between devices, shards(): lax.all_to_all(jnp.stack([w_out] * lax.axis_size(MP)), MP, 0, 0)  184 us
    all_gather x1, waiting for transfers between devices, shards(): lax.all_gather(normed_out, DP_MP, axis=0, tiled=True)  83.9 us
    all_gather x3, blocking collectives, collected_together(): both, at, found = (lax.all_gather(jnp.concatenate(lines), axis), 0, {})  26.1 us
    dot_general x1, matrix products, block_stats(): logits = jnp.dot(normed_rows, columns, preferred_element_type=jnp.float32)  24.1 us
    all_gather x1, blocking collectives, shards(): lax.all_gather(label_rows, DP_MP, axis=0, tiled=True)  21.2 us
    all_to_all x1, blocking collectives, shards(): lax.all_to_all(ctx_rows, MP, split_axis=0, concat_axis=1, tiled=True)  15.7 us
    all_to_all x2, starting transfers between devices, sent_to_all(): return lax.all_to_all(copies, axis, split_axis=0, concat_axis=0, tiled=True)  13.4 us
    dot_general x2, matrix products, project(): jnp.einsum('nd,cde->cne', flat_rows, weights, preferred_element_type=jnp....  9.47 us
  transfers between devices with their start and end apart: 4, of which 3 were waited for; matrix products, arithmetic and copies ran while one was open for 7% of the time, Pallas kernels for 0%

profile of v1, /device:TPU:0, one launch (start us, length us, event | category | flops | bytes accessed | tf_op | source)
XLA Modules:
  0.0 458.2 jit_solution(1393902133105044453)
XLA Ops:
  7.2 3.2 fusion.36
  10.4 3.8 fusion.38
  14.2 1.0 copy.72
  15.2 0.3 reshape.1002
  15.5 3.4 fusion.42
  19.0 0.9 fusion.26
  19.9 6.1 %fusion.39 = f32[3,512,256]{1,2,0:T(8,128)S(1)} fusion(bf16[3,4096,256]{2,1,0:T(8,128)(2,1)} %param.16, bf16[1,512,4096]{2,1,0:T(8,128)(2,1)S(1)} %copy-done.1, f32[4096]{0:T(1024)S(1)} %copy-done.5, f32[512]{0:T(512)S(1)} %add_rsqrt_fusion.1), kind=kOutput, calls=%fused_computation.46 | convolution fusion | flops 3229614080 | bytes 12077056 | tf_op jit(solution)/shard_map/nd,cde->cne/dot_general | solution.py:97
  26.0 0.1 fusion.104
  26.1 0.5 multiply_cosine_fusion
  26.7 0.2 subtract_convert_fusion
  26.9 0.1 copy.84
  27.0 0.1 reshape.1005
  27.1 0.3 multiply_cosine_fusion.1
  27.4 0.1 reshape_squeeze.9
  27.5 0.4 subtract_convert_fusion.2
  27.9 0.3 pad_maximum_fusion.4
  28.2 0.1 copy.83
  28.4 7.3 %while.11 = (s32[]{:T(128)}, bf16[2,1,512,256]{3,2,0,1:T(8,128)(2,1)S(1)}, bf16[2,100,256]{2,1,0:T(8,128)(2,1)S(1)}, bf16[1,512,256]{1,2,0:T(8,128)(2,1)S(1)}, b...) while((s32[]{:T(128)}, ...), condition=%wide.wide.region_5.6_spmd, body=%wide.wide.region_2.5_spmd.sunk | while | flops 488637120 | bytes 5288041 | solution.py:162
  28.4 0.1 copy.116
  28.6 0.3 pad_maximum_fusion.7
  28.9 0.2 iota_compare_fusion.4
  29.1 1.2 fusion.133
  30.3 1.6 fusion.134
  31.9 0.1 copy.117
  32.1 0.1 copy.116
  32.2 0.3 pad_maximum_fusion.7
  32.6 0.2 iota_compare_fusion.4
  32.8 1.2 fusion.133
  34.0 1.6 fusion.134
  35.5 0.1 copy.117
  35.7 15.7 %all_to_all.33 = bf16[8,128,256]{2,1,0:T(8,128)(2,1)} all-to-all(bf16[8,128,256]{2,1,0:T(8,128)(2,1)S(1)} %bitcast.286), channel_id=1, replica_groups=mesh['prompt'=4,'dp'=4,'mp_0'=4,'mp_1'=2] {'mp_0','mp_1'}, dimensions={0} | all-to-all | bytes 1048576 | tf_op jit(solution)/shard_map/all_to_all | solution.py:166
  51.4 6.9 %stack.2 = bf16[8,256,4096]{2,1,0:T(8,128)(2,1)} broadcast(bf16[256,4096]{1,0:T(8,128)(2,1)} %param.17), dimensions={1,2} | broadcast | bytes 18874368 | tf_op jit(solution)/shard_map/stack | solution.py:168
  58.3 5.8 %all-to-all-start.1 = ((bf16[8,256,4096]{2,1,0:T(8,128)(2,1)}), bf16[8,256,4096]{2,1,0:T(8,128)(2,1)}, u32[]{:S(2)}, u32[]{:S(2)}) async-start(bf16[8,256,4096]{2,1,0:T(8,128)(2,1)} %stack.2), calls=%async_computation.1 | async-start | bytes 33554432 | tf_op jit(solution)/shard_map/all_to_all | solution.py:168
  64.0 0.3 all-gather.9.cloned.1.call-start
  64.3 184.2 %all-to-all-done.1 = bf16[8,256,4096]{2,1,0:T(8,128)(2,1)} async-done(((bf16[8,256,4096]{2,1,0:T(8,128)(2,1)}), bf16[8,256,4096]{2,1,0:T(8,128)(2,1)}, u32[]{:S(2)}, u32[]{:S(2)}) %all-to-all-start.1) | async-done | bytes 16777248 | tf_op jit(solution)/shard_map/all_to_all | solution.py:168
  248.5 8.6 %convert_reduce_fusion = f32[128,4096]{1,0:T(8,128)S(1)} fusion(bf16[8,256,4096]{2,1,0:T(8,128)(2,1)} %all-to-all-done.1, bf16[8,128,256]{2,1,0:T(8,128)(2,1)} %all_to_all.33), kind=kOutput, calls=%fused_computation.24 | convolution fusion | flops 2159542272 | bytes 19398656 | tf_op jit(solution)/shard_map/rgk,gkd->rgd/dot_general | solution.py:171
  257.2 4.3 tile.21
  261.5 1.6 multiply_reduce_fusion
  263.1 2.6 multiply_convert_fusion
  266.4 0.6 broadcast_in_dim.64
  267.0 7.0 %all-to-all-start.3 = ((f32[16,1,1]{2,1,0:T(1,128)}), f32[16,1,1]{2,1,0:T(1,128)S(1)}, u32[]{:S(2)}, u32[]{:S(2)}) async-start(f32[16,1,1]{2,1,0:T(1,128)} %broadcast_in_dim.64), calls=%async_computation.3 | async-start | bytes 16384 | tf_op jit(solution)/shard_map/all_to_all | solution.py:54
  274.1 0.1 dynamic-slice_bitcast_fusion
  274.1 21.2 %all-gather.3 = s32[32,1,128]{2,1,0:T(1,128)S(1)} all-gather(s32[1,1,128]{2,1,0:T(1,128)S(1)} %dynamic-slice_bitcast_fusion), channel_id=1, replica_groups=mesh['prompt'=4,'dp'=4,'mp_0'=4,'mp_1'=2] {'dp','mp_0','mp_1'}, dimensions={0}, use_global_device_ids=true | all-gather | bytes 16896 | tf_op jit(solution)/shard_map/all_gather | solution.py:189
  295.4 83.9 %all-gather.9.cloned.1.call-done = bf16[4096,4096]{1,0:T(8,128)(2,1)} async-done(((bf16[128,4096]{1,0:T(8,128)(2,1)}), bf16[4096,4096]{1,0:T(8,128)(2,1)}) %all-gather.9.cloned.1.call-update) | async-done | bytes 33554448 | tf_op jit(solution)/shard_map/all_gather | solution.py:188
  379.3 24.1 %fusion.105 = (f32[4096]{0:T(1024)S(1)}, f32[4096,512]{0,1:T(8,128)}) fusion(bf16[4096,4096]{1,0:T(8,128)(2,1)} %all-gather.9.cloned.1.call-done, bf16[4096,512]{1,0:T(8,128)(2,1)} %param.19), kind=kOutput, calls=%fused_computation.174 | convolution fusion | flops 17181962240 | bytes 46153728 | tf_op jit(solution)/shard_map/dot_general | solution.py:133
  403.4 4.6 exponential_reduce_fusion
  408.0 0.1 maximum_bitcast_fusion
  408.1 12.3 %all-gather.4 = bf16[4,3,4096]{2,1,0:T(4,128)(2,1)S(1)} all-gather(bf16[1,3,4096]{2,1,0:T(4,128)(2,1)S(1)} %maximum_bitcast_fusion), channel_id=2, replica_groups=mesh['prompt'=4,'dp'=4,'mp_0'=4,'mp_1'=2] {'dp'}, dimensions={0}, use_global_device_ids=true | all-gather | bytes 122880 | tf_op jit(solution)/shard_map/all_gather | solution.py:23
  420.4 0.2 maximum_convert_fusion.1
  420.6 0.1 fusion.70
  420.7 0.1 maximum_bitcast_fusion.1
  420.7 12.0 %all-gather.5 = bf16[4,3,4096]{2,1,0:T(4,128)(2,1)S(1)} all-gather(bf16[1,3,4096]{2,1,0:T(4,128)(2,1)S(1)} %maximum_bitcast_fusion.1), channel_id=3, replica_groups=mesh['prompt'=4,'dp'=4,'mp_0'=4,'mp_1'=2] {'mp_0'}, dimensions={0}, use_global_device_ids=true | all-gather | bytes 122880 | tf_op jit(solution)/shard_map/all_gather | solution.py:23
  432.7 0.2 maximum_convert_fusion
  432.9 0.1 fusion.48
  433.0 0.1 maximum_bitcast_fusion.2
  433.1 1.9 all-gather.6
  434.9 0.1 slice_convert_fusion.5
  435.1 0.6 fusion.100
  435.7 0.1 fusion.99
  435.8 0.6 broadcast_in_dim.59
  436.4 6.3 %all-to-all-start.2 = ((f32[16,1,8]{2,1,0:T(1,128)}), f32[16,1,8]{2,1,0:T(1,128)S(1)}, u32[]{:S(2)}, u32[]{:S(2)}) async-start(f32[16,1,8]{2,1,0:T(1,128)} %broadcast_in_dim.59), calls=%async_computation.2 | async-start | bytes 16384 | tf_op jit(solution)/shard_map/all_to_all | solution.py:54
  442.7 0.6 reduce_sum.112
  443.3 6.9 %all-to-all-done.2 = f32[16,1,8]{2,1,0:T(1,128)S(1)} async-done(((f32[16,1,8]{2,1,0:T(1,128)}), f32[16,1,8]{2,1,0:T(1,128)S(1)}, u32[]{:S(2)}, u32[]{:S(2)}) %all-to-all-start.2) | async-done | bytes 544 | tf_op jit(solution)/shard_map/all_to_all | solution.py:54
  450.3 1.1 multiply_divide_fusion
  (50 shorter events, 0.5 us)
Async XLA Ops:
  7.2 266.9 %copy-start = (s32[1,512]{1,0:T(1,128)S(1)}, s32[1,512]{1,0:T(1,128)}, u32[]{:S(2)}) copy-start(s32[1,512]{1,0:T(1,128)} %param.13) | copy-start | bytes 6148
  15.5 3.5 copy-start.1
  18.9 0.9 copy-start.4
  18.9 1.0 copy-start.5
  26.0 1.4 slice-start
  27.0 1.4 copy-start.3
  58.3 190.3 %all-to-all-start.1 = ((bf16[8,256,4096]{2,1,0:T(8,128)(2,1)}), bf16[8,256,4096]{2,1,0:T(8,128)(2,1)}, u32[]{:S(2)}, u32[]{:S(2)}) async-start(bf16[8,256,4096]{2,1,0:T(8,128)(2,1)} %stack.2), calls=%async_computation.1 | async-start | bytes 33554432 | tf_op jit(solution)/shard_map/all_to_all | solution.py:168
  64.0 315.3 %all-gather.9.cloned.1.call-start = ((), (), s32[]{:S(2)}) async-start(), calls=%async_computation.4 | async-start | bytes 34603008 | tf_op jit(solution)/shard_map/all_gather | solution.py:188
  248.5 8.6 %copy-start.2 = (bf16[1,512,4096]{2,1,0:T(8,128)(2,1)S(1)}, bf16[1,512,4096]{2,1,0:T(8,128)(2,1)}, u32[]{:S(2)}) copy-start(bf16[1,512,4096]{2,1,0:T(8,128)(2,1)} %param.12) | copy-start | bytes 12582916
  257.2 5.9 %copy-start.6 = (f32[4096]{0:T(1024)S(1)}, f32[4096]{0:T(1024)}, u32[]{:S(2)}) copy-start(f32[4096]{0:T(1024)} %param.18) | copy-start | bytes 49156
  267.0 168.8 %all-to-all-start.3 = ((f32[16,1,1]{2,1,0:T(1,128)}), f32[16,1,1]{2,1,0:T(1,128)S(1)}, u32[]{:S(2)}, u32[]{:S(2)}) async-start(f32[16,1,1]{2,1,0:T(1,128)} %broadcast_in_dim.64), calls=%async_computation.3 | async-start | bytes 16384 | tf_op jit(solution)/shard_map/all_to_all | solution.py:54
  436.4 13.9 %all-to-all-start.2 = ((f32[16,1,8]{2,1,0:T(1,128)}), f32[16,1,8]{2,1,0:T(1,128)S(1)}, u32[]{:S(2)}, u32[]{:S(2)}) async-start(f32[16,1,8]{2,1,0:T(1,128)} %broadcast_in_dim.59), calls=%async_computation.2 | async-start | bytes 16384 | tf_op jit(solution)/shard_map/all_to_all | solution.py:54
Sparse Core Ops, SparseCore 0:
  265.9 113.4 all-gather.8
